TPU v7x, 32 devices: a whole 2x2x4 slice. The times are simulated.
32 devices in a mesh: grp: 2 (over y), tr: 8 (over z, x), root: 2 (over core).
Axes of the slice: x: 2, y: 2, z: 4, core: 2. Of those that a mesh axis runs over, the one named last changes fastest.
Arguments:
- residual: bfloat16 [128, 65536], P('root', ('grp', 'tr')), parts along dimension 1, may hold values from -8 to 8
- subspace: bfloat16 [512, 65536], P(None, ('grp', 'tr')), parts along dimension 1, may hold values from -1 to 1, as said below
- inverses: bfloat16 [16, 512, 512], P(('grp', 'tr')), parts along dimension 0, may hold values from -1 to 3, as said below
- owner_offset: int32 [128], P(('grp', 'tr')), parts along dimension 0, may hold values from 0 to 3, as said below
- listed: int32 [128], P(('grp', 'tr')), parts along dimension 0, may hold values from 0 to 1, as said below
Outputs:
- corrections: float32 [128, 65536], P('root', ('grp', 'tr')), parts along dimension 1
There are 2 independent parts, one for each index of `grp`. A program takes and returns all parts, laid end to end along the dimension named above; each array names one. Nothing has to cross between parts.
Inputs may be any that keep to these rules, and one draw needn't show every extreme that they name: Each entry of subspace lies within the stated range; rows are not normalized. `inverses`: each inverse is a dense real matrix. `owner_offset`: among the 8 blocks of each shard, at least one is listed and has offset 3. Each shard has at least one listed block and at least one unlisted block.
All inputs are finite; a program needn't handle non-finite values.
Results may differ from a plain program's by a relative error of at most 0.0065.
Values may be sent and summed in bfloat16 or wider, within the bound.
A program may use at most 64 MiB of HBM per device.

v0:
```python
import functools
import jax
import jax.numpy as jnp
from jax import lax
from jax.experimental import pallas as pl
from jax.experimental.pallas import tpu as pltpu
from jax.sharding import PartitionSpec as P

OFFS = 4
PASSES = 2
PARTS = 1
LINK = jnp.bfloat16
SUBLANES = 8
CHUNKS = 4
HOPS = 6
MESH = pl.DeviceIdType.MESH


def each(count, body):
    if count <= 16:
        for i in range(count):
            body(i)
    else:
        pl.loop(0, count)(body)


def kernel(n, roots, off, listed, res, sub, inv, out, table, res_v, sub_v, work, picked,
           partial, inbox, slabs, load_sem, hop_send, hop_recv, swap_send, swap_recv,
           rs_send, rs_recv, ag_send, ag_recv, out_sem):
    me = lax.axis_index("tr")
    root = lax.axis_index("root")
    rows, cols = res.shape
    blk = inv.shape[1]
    blocks = cols // blk
    width = sub.shape[0] // PARTS
    share = blk // roots
    owners = slabs.shape[1]
    base = (n - owners) // 2
    slab = rows // owners

    def block(b):
        return pl.ds(b * blk, blk)

    own_load = pltpu.make_async_copy(inv.at[0], table.at[lax.rem(me, 2)], load_sem.at[0])
    own_load.start()
    res_load = pltpu.make_async_copy(res, res_v, load_sem.at[1])
    res_load.start()
    sub_load = pltpu.make_async_copy(sub, sub_v, load_sem.at[2])
    sub_load.start()

    barrier = pltpu.get_barrier_semaphore()

    def is_owner(device):
        return jnp.logical_and(device >= base, device < base + owners)

    side = lax.rem(me, 2)
    twin = me + 1 - 2 * side

    def linked(d):
        peer = lax.rem(me + d + 1, n)
        close = jnp.logical_or(jnp.logical_or(d + 1 == 2, d + 1 == n - 2), peer == twin)
        return jnp.logical_or(close, jnp.logical_or(is_owner(me), is_owner(peer)))

    def greet(d):
        def signal():
            pl.semaphore_signal(barrier, inc=1, device_id={"tr": lax.rem(me + d + 1, n)}, device_id_type=MESH)

        pl.when(linked(d))(signal)

    each(n - 1, greet)
    for d in range(1, roots):
        pl.semaphore_signal(barrier, inc=1, device_id={"root": lax.rem(root + d, roots)}, device_id_type=MESH)
    partners = lax.fori_loop(0, n - 1, lambda d, c: c + linked(d).astype(jnp.int32), jnp.int32(roots - 1))
    pl.semaphore_wait(barrier, partners)

    chunk = share // CHUNKS

    def chunk_rows(half, q):
        return pl.ds(pl.multiple_of(half * share + q * chunk, chunk), chunk)

    def hop(src, q, slot, peer, sem):
        return pltpu.make_async_remote_copy(
            src_ref=src, dst_ref=table.at[slot, chunk_rows(root, q)],
            send_sem=hop_send.at[sem, q], recv_sem=hop_recv.at[slot, q],
            device_id={"tr": lax.rem(peer + n, n)}, device_id_type=MESH)

    def own_hop(q, slot, peer, sem):
        return hop(inv.at[0, chunk_rows(root, q)], q, slot, peer, sem)

    def relay(e, q, slot, peer, sem):
        return hop(table.at[e, chunk_rows(root, q)], q, slot, peer, sem)

    def swap(e, q, half):
        rows_q = table.at[e, chunk_rows(half, q)]
        return pltpu.make_async_remote_copy(
            src_ref=rows_q, dst_ref=rows_q,
            send_sem=swap_send.at[e, q], recv_sem=swap_recv.at[e, q],
            device_id={"root": 1 - root}, device_id_type=MESH)

    near = me - 2
    roles = {
        (0, 0): ([(2, near)], [(1, [(3, near)], []), (2, [(4, near), (2, twin)], []), (3, [(3, twin)], []), (4, [(4, twin)], [])]),
        (1, 1): ([(3, near)], [(0, [(2, near)], []), (3, [(3, twin)], [(1, twin)]), (2, [(4, near), (2, twin)], []), (4, [], [])]),
        (1, 0): ([(1, twin)], [(2, [], []), (3, [], []), (4, [], [])]),
        (0, 1): ([(0, twin)], [(1, [], []), (3, [], []), (2, [], [])]),
    }

    def per_role(body):
        for (s, r), (own, events) in roles.items():
            pl.when(jnp.logical_and(side == s, root == r))(functools.partial(body, s, own, events))

    def sem_of(events, i, j):
        return 1 + sum(len(targets) + len(late) for _, targets, late in events[:i]) + j

    def open_hops(s, own, events):
        for j, (slot, peer) in enumerate(own):
            for q in range(CHUNKS):
                own_hop(q, slot, peer, j).start()

    def run_events(first, s, own, events):
        cut = len(events) - 1
        for i, (e, targets, late) in enumerate(events):
            if (i < cut) != first:
                continue
            for q in range(CHUNKS):
                relay(e, q, e, twin, 0).wait_recv()
                for j, (slot, peer) in enumerate(targets):
                    relay(e, q, slot, peer, sem_of(events, i, j)).start()
                for j, (slot, peer) in enumerate(late):
                    own_hop(q, slot, peer, sem_of(events, i, len(targets) + j)).start()
                if s < e < s + OFFS:
                    swap(e, q, root).start()

    def close_hops(s, own, events):
        for j, (slot, peer) in enumerate(own):
            for q in range(CHUNKS):
                own_hop(q, slot, peer, j).wait_send()
        for i, (e, targets, late) in enumerate(events):
            for q in range(CHUNKS):
                for j, (slot, peer) in enumerate(targets):
                    relay(e, q, slot, peer, sem_of(events, i, j)).wait_send()
                for j, (slot, peer) in enumerate(late):
                    own_hop(q, slot, peer, sem_of(events, i, len(targets) + j)).wait_send()
                if s < e < s + OFFS:
                    swap(e, q, root).wait_send()

    per_role(open_hops)

    res_load.wait()
    for b in range(blocks):
        kept = jnp.where(listed[b] > 0, 0.0, res_v[:, block(b)].astype(jnp.float32))
        work[:, block(b)] = kept

    def apply(o):
        for b in range(blocks):
            hit = jnp.logical_and(listed[b] > 0, off[b] == o)
            x = res_v[:, block(b)].astype(jnp.float32)
            picked[pl.ds(b * rows, rows), :] = jnp.where(hit, x, 0.0).astype(jnp.bfloat16)
        for b in range(blocks):
            part = jnp.dot(picked[pl.ds(b * rows, rows), :], table[side + o], preferred_element_type=jnp.float32)
            work[:, block(b)] += part

    def arrive_and_apply(o):
        for q in range(CHUNKS):
            swap(side + o, q, 1 - root).wait_recv()
        apply(o)

    own_load.wait()
    apply(0)
    per_role(functools.partial(run_events, True))
    arrive_and_apply(1)
    per_role(functools.partial(run_events, False))
    for o in range(2, OFFS):
        arrive_and_apply(o)
    sub_load.wait()

    def rs_copy(i, j):
        return pltpu.make_async_remote_copy(
            src_ref=partial.at[i, j], dst_ref=inbox.at[i, me],
            send_sem=rs_send.at[i, j], recv_sem=rs_recv.at[i, me],
            device_id={"tr": base + j}, device_id_type=MESH)

    def rs_in(i, peer):
        return pltpu.make_async_remote_copy(
            src_ref=inbox.at[i, peer], dst_ref=inbox.at[i, peer],
            send_sem=rs_send.at[i, 0], recv_sem=rs_recv.at[i, peer],
            device_id={"tr": peer}, device_id_type=MESH)

    def ag_copy(i, d):
        return pltpu.make_async_remote_copy(
            src_ref=slabs.at[i, me - base], dst_ref=slabs.at[i, me - base],
            send_sem=ag_send.at[i, d], recv_sem=ag_recv.at[i, me - base],
            device_id={"tr": lax.rem(me + d + 1, n)}, device_id_type=MESH)

    def ag_in(i, j):
        return pltpu.make_async_remote_copy(
            src_ref=slabs.at[i, j], dst_ref=slabs.at[i, j],
            send_sem=ag_send.at[i, 0], recv_sem=ag_recv.at[i, j],
            device_id={"tr": base + j}, device_id_type=MESH)

    def span(h):
        return pl.ds(h * width, width)

    def for_other_owners(body):
        for j in range(owners):
            pl.when(me != base + j)(functools.partial(body, j))

    for k in range(PASSES):
        for b in range(blocks):
            res_v[:, block(b)] = work[:, block(b)].astype(jnp.bfloat16)
        for h in range(PARTS):
            i = k * PARTS + h
            total = jnp.zeros((rows, width), jnp.float32)
            for b in range(blocks):
                total += lax.dot_general(
                    res_v[:, block(b)], sub_v[span(h), block(b)],
                    (((1,), (1,)), ((), ())), preferred_element_type=jnp.float32)
            partial[i] = total.reshape(owners, slab, width).astype(partial.dtype)

            for_other_owners(lambda j: rs_copy(i, j).start())

        def own_sum(i):
            inbox[i, me] = partial[i, me - base]
            each(n - 1, lambda d: rs_in(i, lax.rem(me + d + 1, n)).wait_recv())
            slabs[i, me - base] = jnp.sum(inbox[i].astype(jnp.float32), axis=0).astype(jnp.bfloat16)
            each(n - 1, lambda d: ag_copy(i, d).start())

        for h in range(PARTS):
            pl.when(is_owner(me))(functools.partial(own_sum, k * PARTS + h))
        for h in range(PARTS):
            i = k * PARTS + h
            for_other_owners(lambda j: ag_in(i, j).wait_recv())
            coef = jnp.concatenate(
                [slabs[i, j].astype(jnp.float32) for j in range(owners)], axis=0).astype(jnp.bfloat16)
            for b in range(blocks):
                work[:, block(b)] -= jnp.dot(
                    coef, sub_v[span(h), block(b)], preferred_element_type=jnp.float32)
                if i == PASSES * PARTS - 1:
                    pltpu.make_async_copy(work.at[:, block(b)], out.at[:, block(b)], out_sem.at[b]).start()

    per_role(close_hops)
    for i in range(PASSES * PARTS):
        for_other_owners(lambda j: rs_copy(i, j).wait_send())

        def sent():
            each(n - 1, lambda d: ag_copy(i, d).wait_send())

        pl.when(is_owner(me))(sent)
    for b in range(blocks):
        pltpu.make_async_copy(work.at[:, block(b)], out.at[:, block(b)], out_sem.at[b]).wait()


def per_device(n, roots, residual, subspace, inverses, owner_offset, listed):
    rows, cols = residual.shape
    spans = subspace.shape[0]
    blk = inverses.shape[1]
    blocks = cols // blk
    owners = min(n // 2, rows // SUBLANES)
    slab = rows // owners
    rounds = PASSES * PARTS
    hbm = pl.BlockSpec(memory_space=pl.ANY)
    smem = pl.BlockSpec(memory_space=pltpu.SMEM)
    dma = pltpu.SemaphoreType.DMA
    return pl.pallas_call(
        functools.partial(kernel, n, roots),
        out_shape=jax.ShapeDtypeStruct((rows, cols), jnp.float32),
        in_specs=[smem, smem, hbm, hbm, hbm],
        out_specs=hbm,
        scratch_shapes=[
            pltpu.VMEM((OFFS + 1, blk, blk), jnp.bfloat16),
            pltpu.VMEM((rows, cols), jnp.bfloat16),
            pltpu.VMEM((spans, cols), jnp.bfloat16),
            pltpu.VMEM((rows, cols), jnp.float32),
            pltpu.VMEM((blocks * rows, blk), jnp.bfloat16),
            pltpu.VMEM((rounds, owners, slab, spans // PARTS), LINK),
            pltpu.VMEM((rounds, n, slab, spans // PARTS), LINK),
            pltpu.VMEM((rounds, owners, slab, spans // PARTS), jnp.bfloat16),
            dma((3,)),
            dma((HOPS, CHUNKS)), dma((OFFS + 1, CHUNKS)),
            dma((OFFS + 1, CHUNKS)), dma((OFFS + 1, CHUNKS)),
            dma((rounds, owners)), dma((rounds, n)),
            dma((rounds, n)), dma((rounds, owners)),
            dma((blocks,)),
        ],
        compiler_params=pltpu.CompilerParams(collective_id=0, has_side_effects=True),
    )(owner_offset, listed, residual, subspace, inverses)


def solution(mesh):
    body = functools.partial(per_device, mesh.shape["tr"], mesh.shape["root"])
    return jax.shard_map(
        body,
        mesh=mesh,
        in_specs=(
            P("root", ("grp", "tr")),
            P(None, ("grp", "tr")),
            P(("grp", "tr"), None, None),
            P(("grp", "tr")),
            P(("grp", "tr")),
        ),
        out_specs=P("root", ("grp", "tr")),
        check_vma=False,
    )
```

profile of v0, /device:TPU:0, one launch (start us, length us, event | category | flops | bytes accessed | tf_op | source)
XLA Modules:
  0.0 50.4 jit_solution(18101628483119532898)
XLA Ops:
  0.0 48.1 %shard_map.55 = f32[64,4096]{1,0:T(8,128)} custom-call(s32[8]{0:T(128)} %off.1, s32[8]{0:T(128)} %listed.1, bf16[64,4096]{1,0:T(8,128)(2,1)} %res.1, bf16[512,4096]{1,0:T(8,128)(2,1)} %sub.1, bf16[1,512,512]{2,1,0:T(8,128)(2,1)} %inv.1), custom_call_target="tpu_custom_call" | custom-call | tf_op jit(solution)/shard_map/pallas_call | solution.py:264
  48.1 2.3 %copy.7 = f32[64,4096]{1,0:T(8,128)} copy(f32[64,4096]{1,0:T(8,128)} %shard_map.55) | data formatting | bytes 2097152
where the time goes:
time: 50.5 us; the launch traced here: 50.4 us
  Pallas kernels  48.1 us (95%)
  local copies, waits for them, and re-layouts  2.27 us (4%)
    pallas_call x1, Pallas kernels, per_device(): pl.pallas_call(functools.partial(kernel, n, roots), out_shape=jax.ShapeDt...  48.1 us
    unnamed x1, local copies, waits for them, and re-layouts  2.27 us

commit v1 on v0

v1 whole, which is shorter than its diff:
```python
import functools
import jax
import jax.numpy as jnp
from jax import lax
from jax.experimental import pallas as pl
from jax.experimental.pallas import tpu as pltpu
from jax.sharding import PartitionSpec as P

OFFS = 4
PASSES = 2
LINK = jnp.bfloat16
SUBLANES = 8
CHUNKS = 8
EARLY = 3
MESH = pl.DeviceIdType.MESH
VMEM_GRANT = 61_700_000


def each(count, body):
    if count <= 16:
        for i in range(count):
            body(i)
    else:
        pl.loop(0, count)(body)


def flows(side):
    every, early, late = range(CHUNKS), range(EARLY), range(EARLY, CHUNKS)
    if side == 0:
        own = [(every, 2, "near"), ]
        order = []
        for q in every:
            order.append((2, q, [(1, "twin")]))
            if q in early:
                order.append((1, q, [(3, "near")]))
        order += [(1, q, []) for q in late]
        order += [(3, q, [(2, "twin")]) for q in early]
        order += [(3, q, []) for q in late]
    else:
        own = [(every, 1, "twin"), (late, 2, "near")]
        order = [(2, q, [(3, "twin")]) for q in late]
        order += [(1, q, [(3, "near")]) for q in every]
        order += [(2, q, []) for q in early]
        order += [(3, q, []) for q in every]
    return own, order


def dot_t(a, b):
    return lax.dot_general(a, b, (((1,), (1,)), ((), ())), preferred_element_type=jnp.float32)


def kernel(n, roots, off, listed, res, sub, inv, work, sub_v, coef, table, res_v, gram_sum, gram_hi, gram_lo, corr,
           partial, inbox, slabs, load_sem, hop_send, hop_recv, swap_send, swap_recv,
           rs_send, rs_recv, ag_send, ag_recv):
    me = lax.axis_index("tr")
    root = lax.axis_index("root")
    rows, cols = res.shape
    blk = inv.shape[1]
    spans = sub.shape[0]
    blocks = cols // blk
    share = blk // roots
    owners = slabs.shape[1]
    base = (n - owners) // 2
    slab = rows // owners
    chunk = share // CHUNKS

    def block(b):
        return pl.ds(b * blk, blk)

    own_load = pltpu.make_async_copy(inv.at[0], table.at[0], load_sem.at[0])
    res_load = pltpu.make_async_copy(res, res_v, load_sem.at[1])
    sub_load = pltpu.make_async_copy(sub, sub_v, load_sem.at[2])
    sub_load.start()
    own_load.start()
    res_load.start()

    def is_owner(device):
        return jnp.logical_and(device >= base, device < base + owners)

    side = lax.rem(me, 2)
    twin = me + 1 - 2 * side
    peers = {"twin": twin, "near": lax.rem(me + n - 2, n)}

    barrier = pltpu.get_barrier_semaphore()

    def linked(d):
        peer = lax.rem(me + d + 1, n)
        close = jnp.logical_or(jnp.logical_or(d + 1 == 2, d + 1 == n - 2), peer == twin)
        return jnp.logical_or(close, jnp.logical_or(is_owner(me), is_owner(peer)))

    def greet(d):
        def signal():
            pl.semaphore_signal(barrier, inc=1, device_id={"tr": lax.rem(me + d + 1, n)}, device_id_type=MESH)

        pl.when(linked(d))(signal)

    for d in range(1, roots):
        pl.semaphore_signal(barrier, inc=1, device_id={"root": lax.rem(root + d, roots)}, device_id_type=MESH)
    each(n - 1, greet)
    partners = lax.fori_loop(0, n - 1, lambda d, c: c + linked(d).astype(jnp.int32), jnp.int32(roots - 1))
    pl.semaphore_wait(barrier, partners)

    def chunk_rows(half, q):
        return pl.ds(pl.multiple_of(half * share + q * chunk, chunk), chunk)

    def hop(src, q, slot, peer, sem):
        return pltpu.make_async_remote_copy(
            src_ref=src, dst_ref=table.at[slot, chunk_rows(root, q)],
            send_sem=hop_send.at[sem, q], recv_sem=hop_recv.at[slot, q],
            device_id={"tr": peers[peer]}, device_id_type=MESH)

    def own_hop(q, slot, peer, sem):
        return hop(inv.at[0, chunk_rows(root, q)], q, slot, peer, sem)

    def relay(e, q, slot, peer, sem):
        return hop(table.at[e, chunk_rows(root, q)], q, slot, peer, sem)

    def swap(e, q, half):
        rows_q = table.at[e, chunk_rows(half, q)]
        return pltpu.make_async_remote_copy(
            src_ref=rows_q, dst_ref=rows_q,
            send_sem=swap_send.at[e, q], recv_sem=swap_recv.at[e, q],
            device_id={"root": 1 - root}, device_id_type=MESH)

    def gram(b):
        part = dot_t(sub_v[:, block(b)], sub_v[:, block(b)])
        gram_sum[...] = part if b == 0 else gram_sum[...] + part

    def exchange(s):
        own, order = flows(s)
        steps = list(range(blocks))
        for j, (chunks, slot, peer) in enumerate(own):
            for q in chunks:
                own_hop(q, slot, peer, j).start()
        sub_load.wait()
        for i, (e, q, targets) in enumerate(order):
            if i % 2 == 0 and steps:
                gram(steps.pop(0))
            relay(e, q, e, "twin", 0).wait_recv()
            for slot, peer in targets:
                relay(e, q, slot, peer, 1 + e).start()
            swap(e, q, root).start()
        for b in steps:
            gram(b)

    def close(s):
        own, order = flows(s)
        for j, (chunks, slot, peer) in enumerate(own):
            for q in chunks:
                own_hop(q, slot, peer, j).wait_send()
        for e, q, targets in order:
            for slot, peer in targets:
                relay(e, q, slot, peer, 1 + e).wait_send()
            swap(e, q, root).wait_send()

    for s in range(2):
        pl.when(side == s)(functools.partial(exchange, s))
    high = gram_sum[...].astype(jnp.bfloat16)
    gram_hi[...] = high
    gram_lo[...] = (gram_sum[...] - high.astype(jnp.float32)).astype(jnp.bfloat16)
    own_load.wait()
    res_load.wait()
    for e in range(1, OFFS):
        for q in range(CHUNKS):
            swap(e, q, 1 - root).wait_recv()

    total = jnp.zeros((rows, spans), jnp.float32)
    for b in range(blocks):
        x = res_v[:, block(b)]
        solved = jnp.dot(x, table[off[b]], preferred_element_type=jnp.float32)
        kept = jnp.where(listed[b] > 0, solved, x.astype(jnp.float32))
        work[:, block(b)] = kept
        total += dot_t(kept.astype(jnp.bfloat16), sub_v[:, block(b)])
    corr[...] = total

    def rs_copy(i, j):
        return pltpu.make_async_remote_copy(
            src_ref=partial.at[i, j], dst_ref=inbox.at[i, me],
            send_sem=rs_send.at[i, j], recv_sem=rs_recv.at[i, me],
            device_id={"tr": base + j}, device_id_type=MESH)

    def rs_in(i, peer):
        return pltpu.make_async_remote_copy(
            src_ref=inbox.at[i, peer], dst_ref=inbox.at[i, peer],
            send_sem=rs_send.at[i, 0], recv_sem=rs_recv.at[i, peer],
            device_id={"tr": peer}, device_id_type=MESH)

    def ag_copy(i, d):
        return pltpu.make_async_remote_copy(
            src_ref=slabs.at[i, me - base], dst_ref=slabs.at[i, me - base],
            send_sem=ag_send.at[i, d], recv_sem=ag_recv.at[i, me - base],
            device_id={"tr": lax.rem(me + d + 1, n)}, device_id_type=MESH)

    def ag_in(i, j):
        return pltpu.make_async_remote_copy(
            src_ref=slabs.at[i, j], dst_ref=slabs.at[i, j],
            send_sem=ag_send.at[i, 0], recv_sem=ag_recv.at[i, j],
            device_id={"tr": base + j}, device_id_type=MESH)

    def for_other_owners(body):
        for j in range(owners):
            pl.when(me != base + j)(functools.partial(body, j))

    def own_sum(i):
        inbox[i, me] = partial[i, me - base]
        each(n - 1, lambda d: rs_in(i, lax.rem(me + d + 1, n)).wait_recv())
        slabs[i, me - base] = jnp.sum(inbox[i].astype(jnp.float32), axis=0).astype(jnp.bfloat16)
        each(n - 1, lambda d: ag_copy(i, d).start())

    def reduce(i, total, cover):
        partial[i] = total.reshape(owners, slab, spans).astype(partial.dtype)
        for_other_owners(lambda j: rs_copy(i, j).start())
        pl.when(is_owner(me))(functools.partial(own_sum, i))
        cover()
        for_other_owners(lambda j: ag_in(i, j).wait_recv())
        return jnp.concatenate(
            [slabs[i, j].astype(jnp.float32) for j in range(owners)], axis=0).astype(jnp.bfloat16)

    first = reduce(0, total, lambda: None)
    total = corr[...] - (
        jnp.dot(first, gram_hi[...], preferred_element_type=jnp.float32)
        + jnp.dot(first, gram_lo[...], preferred_element_type=jnp.float32))

    def update():
        for b in range(blocks):
            work[:, block(b)] -= jnp.dot(first, sub_v[:, block(b)], preferred_element_type=jnp.float32)

    coef[...] = reduce(1, total, update)

    for s in range(2):
        pl.when(side == s)(functools.partial(close, s))
    for i in range(PASSES):
        for_other_owners(lambda j: rs_copy(i, j).wait_send())

        def sent():
            each(n - 1, lambda d: ag_copy(i, d).wait_send())

        pl.when(is_owner(me))(sent)


def finish(blk, work, sub_v, coef, out, out_v, out_sem):
    blocks = work.shape[1] // blk

    def store(b):
        cols = pl.ds(b * blk, blk)
        return pltpu.make_async_copy(out_v.at[:, cols], out.at[:, cols], out_sem.at[b])

    for b in range(blocks):
        cols = pl.ds(b * blk, blk)
        out_v[:, cols] = work[:, cols] - jnp.dot(coef[...], sub_v[:, cols], preferred_element_type=jnp.float32)
        store(b).start()
    for b in range(blocks):
        store(b).wait()


def per_device(n, roots, residual, subspace, inverses, owner_offset, listed):
    rows, cols = residual.shape
    spans = subspace.shape[0]
    blk = inverses.shape[1]
    blocks = cols // blk
    owners = min(n // 2, rows // SUBLANES)
    slab = rows // owners
    hbm = pl.BlockSpec(memory_space=pl.ANY)
    smem = pl.BlockSpec(memory_space=pltpu.SMEM)
    vmem = pl.BlockSpec(memory_space=pltpu.VMEM)
    dma = pltpu.SemaphoreType.DMA
    held = pl.pallas_call(
        functools.partial(kernel, n, roots),
        out_shape=(
            pltpu.VMEM((rows, cols), jnp.float32),
            pltpu.VMEM((spans, cols), jnp.bfloat16),
            pltpu.VMEM((rows, spans), jnp.bfloat16),
        ),
        in_specs=[smem, smem, hbm, hbm, hbm],
        out_specs=(vmem, vmem, vmem),
        scratch_shapes=[
            pltpu.VMEM((OFFS, blk, blk), jnp.bfloat16),
            pltpu.VMEM((rows, cols), jnp.bfloat16),
            pltpu.VMEM((spans, spans), jnp.float32),
            pltpu.VMEM((spans, spans), jnp.bfloat16),
            pltpu.VMEM((spans, spans), jnp.bfloat16),
            pltpu.VMEM((rows, spans), jnp.float32),
            pltpu.VMEM((PASSES, owners, slab, spans), LINK),
            pltpu.VMEM((PASSES, n, slab, spans), LINK),
            pltpu.VMEM((PASSES, owners, slab, spans), jnp.bfloat16),
            dma((3,)),
            dma((1 + OFFS, CHUNKS)), dma((OFFS, CHUNKS)),
            dma((OFFS, CHUNKS)), dma((OFFS, CHUNKS)),
            dma((PASSES, owners)), dma((PASSES, n)),
            dma((PASSES, n)), dma((PASSES, owners)),
        ],
        compiler_params=pltpu.CompilerParams(
            collective_id=0, has_side_effects=True, vmem_limit_bytes=VMEM_GRANT),
    )(owner_offset, listed, residual, subspace, inverses)
    return pl.pallas_call(
        functools.partial(finish, blk),
        out_shape=jax.ShapeDtypeStruct((rows, cols), jnp.float32),
        in_specs=[vmem, vmem, vmem],
        out_specs=hbm,
        scratch_shapes=[pltpu.VMEM((rows, cols), jnp.float32), dma((blocks,))],
        compiler_params=pltpu.CompilerParams(vmem_limit_bytes=16 * 2**20),
    )(*held)


def solution(mesh):
    body = functools.partial(per_device, mesh.shape["tr"], mesh.shape["root"])
    return jax.shard_map(
        body,
        mesh=mesh,
        in_specs=(
            P("root", ("grp", "tr")),
            P(None, ("grp", "tr")),
            P(("grp", "tr"), None, None),
            P(("grp", "tr")),
            P(("grp", "tr")),
        ),
        out_specs=P("root", ("grp", "tr")),
        check_vma=False,
    )
```

time: 50.5 us -> 43.2 us (0.86)
  Pallas kernels: 48.1 us -> 43.1 us
  local copies, waits for them, and re-layouts: 2.27 us -> 0 us
    pallas_call x1 -> x2, Pallas kernels: 48.1 us -> 43.1 us  [the longest x1 41.5 us: per_device(): pl.pallas_call(functools.partial(kernel, n, roots), out_shape=(pltpu.VMEM...]
    unnamed x1 -> x0, local copies, waits for them, and re-layouts: 2.27 us -> none
where the time goes in v1:
time: 43.2 us; the launch traced here: 43.1 us
  Pallas kernels  43.1 us (100%)
    pallas_call x1, Pallas kernels, per_device(): pl.pallas_call(functools.partial(kernel, n, roots), out_shape=(pltpu.VMEM...  41.5 us
    pallas_call x1, Pallas kernels, per_device(): pl.pallas_call(functools.partial(finish, blk), out_shape=jax.ShapeDtypeSt...  1.57 us

profile of v1, /device:TPU:0, one launch (start us, length us, event | category | flops | bytes accessed | tf_op | source)
XLA Modules:
  0.0 43.1 jit_solution(17900286281904144552)
XLA Ops:
  0.0 41.5 %shard_map.55 = (f32[64,4096]{1,0:T(8,128)S(1)}, bf16[512,4096]{1,0:T(8,128)(2,1)S(1)}, bf16[64,512]{1,0:T(8,128)(2,1)S(1)}) custom-call(s32[8]{0:T(128)} %off.1, s32[8]{0:T(128)} %listed.1, bf16[64,4096]{1,0:T(8,128)(2,1)} %res.1, bf16[512,4096]{1,0:T(8,128)(2,1)} %sub.1, bf16[1,512,512]{2,1,0:T(8,128)(2,1)} %inv.1), custom_call_target="tpu_custom_call" | custom-call | tf_op jit(solution)/shard_map/pallas_call | solution.py:267
  41.5 1.6 %shard_map.56 = f32[64,4096]{1,0:T(8,128)} custom-call(f32[64,4096]{1,0:T(8,128)S(1)} %get-tuple-element.8.work, bf16[512,4096]{1,0:T(8,128)(2,1)S(1)} %get-tuple-element.9.sub_v, bf16[64,512]{1,0:T(8,128)(2,1)S(1)} %get-tuple-element.10.coef), custom_call_target="tpu_custom_call" | custom-call | tf_op jit(solution)/shard_map/pallas_call | solution.py:295

commit v2 on v1

--- a/solution.py
+++ b/solution.py
@@ -10,8 +10,11 @@
 PASSES = 2
 LINK = jnp.bfloat16
 SUBLANES = 8
+LANES = 128
 CHUNKS = 8
 EARLY = 3
+TREE_AT = 19
+TWINS_AT = 26
 MESH = pl.DeviceIdType.MESH
 VMEM_GRANT = 61_700_000
 
@@ -50,8 +53,9 @@
 
 
 def kernel(n, roots, off, listed, res, sub, inv, work, sub_v, coef, table, res_v, gram_sum, gram_hi, gram_lo, corr,
-           partial, inbox, slabs, load_sem, hop_send, hop_recv, swap_send, swap_recv,
-           rs_send, rs_recv, ag_send, ag_recv):
+           partial, inbox, slabs, strips, diag_out, diag_in, diag, tree_out, tree_in,
+           load_sem, hop_send, hop_recv, swap_send, swap_recv, rs_send, rs_recv, ag_send, ag_recv,
+           tree_send, tree_recv, diag_send, diag_recv, pair_send, pair_recv):
     me = lax.axis_index("tr")
     root = lax.axis_index("root")
     rows, cols = res.shape
@@ -61,8 +65,10 @@
     share = blk // roots
     owners = slabs.shape[1]
     base = (n - owners) // 2
-    slab = rows // owners
+    width = spans // owners
     chunk = share // CHUNKS
+    shared = strips is not None
+    half = spans // roots
 
     def block(b):
         return pl.ds(b * blk, blk)
@@ -122,26 +128,112 @@
             send_sem=swap_send.at[e, q], recv_sem=swap_recv.at[e, q],
             device_id={"root": 1 - root}, device_id_type=MESH)
 
-    def gram(b):
-        part = dot_t(sub_v[:, block(b)], sub_v[:, block(b)])
+    def gram_step(b):
+        mine = sub_v[pl.ds(pl.multiple_of(root * half, half), half), block(b)] if shared else sub_v[:, block(b)]
+        part = dot_t(sub_v[:, block(b)], mine)
         gram_sum[...] = part if b == 0 else gram_sum[...] + part
+
+    lower = me < n // 2
+    toward = jnp.where(lower, me + 2, me - 2)
+
+    def strip(k, beside=False):
+        owner = (1 - side if beside else side) + 2 * k
+        return pl.ds(pl.multiple_of(owner * width, width), width)
+
+    def tree_copy(k, peer):
+        return pltpu.make_async_remote_copy(
+            src_ref=tree_out.at[k], dst_ref=tree_in.at[k], send_sem=tree_send.at[k], recv_sem=tree_recv.at[k],
+            device_id={"tr": peer}, device_id_type=MESH)
+
+    def diag_copy(t):
+        return pltpu.make_async_remote_copy(
+            src_ref=diag_out.at[t], dst_ref=diag_in.at[me], send_sem=diag_send.at[t], recv_sem=diag_recv.at[me],
+            device_id={"tr": base + 2 * root + t}, device_id_type=MESH)
+
+    def diag_from(peer):
+        return pltpu.make_async_remote_copy(
+            src_ref=diag_out.at[0], dst_ref=diag_in.at[peer], send_sem=diag_send.at[0], recv_sem=diag_recv.at[peer],
+            device_id={"tr": peer}, device_id_type=MESH)
+
+    def pair_copy(ref, k):
+        return pltpu.make_async_remote_copy(
+            src_ref=ref, dst_ref=ref, send_sem=pair_send.at[k], recv_sem=pair_recv.at[k],
+            device_id={"root": 1 - root}, device_id_type=MESH)
+
+    def for_own_diag(body):
+        for t in range(2):
+            pl.when(me != base + 2 * root + t)(functools.partial(body, t))
+
+    def start_tree():
+        shape = (width, width)
+        on = lax.broadcasted_iota(jnp.int32, shape, 0) == lax.broadcasted_iota(jnp.int32, shape, 1)
+        for t in range(2):
+            place = pl.ds(pl.multiple_of((2 * root + t) * width, width), width)
+            span = pl.ds(t * width, width)
+            square = gram_sum[place, span]
+            line = jnp.sum(jnp.where(on, square, 0.0), axis=0, keepdims=True)
+            diag_out[t] = jnp.broadcast_to(line, diag_out.shape[1:])
+            gram_sum[place, span] = jnp.where(on, 0.0, square)
+        for k in range(2):
+            tree_out[k] = gram_sum[strip(k, beside=True), :].astype(LINK)
+            tree_copy(k, twin).start()
+        for_own_diag(lambda t: diag_copy(t).start())
+
+    def sum_twins():
+        for k in range(2):
+            tree_copy(k, twin).wait_recv()
+            gram_sum[strip(k), :] += tree_in[k].astype(jnp.float32)
+
+        def outer():
+            for k in range(2):
+                tree_out[2 + k] = gram_sum[strip(k), :].astype(LINK)
+                tree_copy(2 + k, toward).start()
+
+        pl.when(jnp.logical_not(is_owner(me)))(outer)
+
+    def sum_outer():
+        for k in range(2):
+            tree_copy(2 + k, toward).wait_recv()
+            gram_sum[strip(k), :] += tree_in[2 + k].astype(jnp.float32)
+        far = pl.ds(pl.multiple_of((side + 2 * lower.astype(jnp.int32)) * width, width), width)
+        tree_out[4] = gram_sum[far, :].astype(LINK)
+        tree_copy(4, toward).start()
+
+    def sum_inner():
+        tree_copy(4, toward).wait_recv()
+        near = pl.ds(pl.multiple_of((me - base) * width, width), width)
+        strips[root] = (gram_sum[near, :] + tree_in[4].astype(jnp.float32)).astype(LINK)
+        pair_copy(strips.at[root], 0).start()
+
+        def sum_diag():
+            diag_in[me] = diag_out[lax.rem(me - base, 2)]
+            each(n - 1, lambda d: diag_from(lax.rem(me + d + 1, n)).wait_recv())
+            diag[...] = jnp.sum(diag_in[...], axis=0)
+            pair_copy(diag, 1).start()
+
+        pl.when((me - base) // 2 == root)(sum_diag)
+
+    def paired():
+        pair_copy(strips.at[1 - root], 0).wait_recv()
+        pl.when((me - base) // 2 != root)(lambda: pair_copy(diag, 1).wait_recv())
 
     def exchange(s):
         own, order = flows(s)
-        steps = list(range(blocks))
         for j, (chunks, slot, peer) in enumerate(own):
             for q in chunks:
                 own_hop(q, slot, peer, j).start()
         sub_load.wait()
         for i, (e, q, targets) in enumerate(order):
-            if i % 2 == 0 and steps:
-                gram(steps.pop(0))
+            if i < blocks:
+                gram_step(i)
+            if shared and i == TREE_AT:
+                start_tree()
+            if shared and i == TWINS_AT:
+                sum_twins()
             relay(e, q, e, "twin", 0).wait_recv()
             for slot, peer in targets:
                 relay(e, q, slot, peer, 1 + e).start()
             swap(e, q, root).start()
-        for b in steps:
-            gram(b)
 
     def close(s):
         own, order = flows(s)
@@ -155,9 +247,12 @@
 
     for s in range(2):
         pl.when(side == s)(functools.partial(exchange, s))
-    high = gram_sum[...].astype(jnp.bfloat16)
-    gram_hi[...] = high
-    gram_lo[...] = (gram_sum[...] - high.astype(jnp.float32)).astype(jnp.bfloat16)
+    if shared:
+        pass
+    else:
+        high = gram_sum[...].astype(jnp.bfloat16)
+        gram_hi[...] = high
+        gram_lo[...] = (gram_sum[...] - high.astype(jnp.float32)).astype(jnp.bfloat16)
     own_load.wait()
     res_load.wait()
     for e in range(1, OFFS):
@@ -171,7 +266,8 @@
         kept = jnp.where(listed[b] > 0, solved, x.astype(jnp.float32))
         work[:, block(b)] = kept
         total += dot_t(kept.astype(jnp.bfloat16), sub_v[:, block(b)])
-    corr[...] = total
+        if shared and b == TWINS_AT - 3 * CHUNKS:
+            sum_twins()
 
     def rs_copy(i, j):
         return pltpu.make_async_remote_copy(
@@ -201,41 +297,85 @@
         for j in range(owners):
             pl.when(me != base + j)(functools.partial(body, j))
 
+    def send_slab(i, value):
+        slabs[i, me - base] = value
+        each(n - 1, lambda d: ag_copy(i, d).start())
+
     def own_sum(i):
+        if shared:
+            sum_outer()
         inbox[i, me] = partial[i, me - base]
         each(n - 1, lambda d: rs_in(i, lax.rem(me + d + 1, n)).wait_recv())
-        slabs[i, me - base] = jnp.sum(inbox[i].astype(jnp.float32), axis=0).astype(jnp.bfloat16)
-        each(n - 1, lambda d: ag_copy(i, d).start())
-
-    def reduce(i, total, cover):
-        partial[i] = total.reshape(owners, slab, spans).astype(partial.dtype)
+        total = jnp.sum(inbox[i].astype(jnp.float32), axis=0)
+        send_slab(i, total.astype(jnp.bfloat16))
+        if shared:
+            sum_inner()
+            arrive(i)
+            first = gathered(i)
+            paired()
+            again = sum(
+                dot_t(first[:, h * half:(h + 1) * half], strips[h]) for h in range(roots))
+            own = slabs[i, me - base].astype(jnp.float32)
+            send_slab(i + 1, (total - (again + own * diag[pl.ds(0, 1), :])).astype(jnp.bfloat16))
+
+    def scatter(i, total):
+        for j in range(owners):
+            partial[i, j] = total[:, j * width:(j + 1) * width].astype(partial.dtype)
         for_other_owners(lambda j: rs_copy(i, j).start())
         pl.when(is_owner(me))(functools.partial(own_sum, i))
-        cover()
+
+    def arrive(i):
         for_other_owners(lambda j: ag_in(i, j).wait_recv())
-        return jnp.concatenate(
-            [slabs[i, j].astype(jnp.float32) for j in range(owners)], axis=0).astype(jnp.bfloat16)
-
-    first = reduce(0, total, lambda: None)
-    total = corr[...] - (
-        jnp.dot(first, gram_hi[...], preferred_element_type=jnp.float32)
-        + jnp.dot(first, gram_lo[...], preferred_element_type=jnp.float32))
-
-    def update():
+
+    def gathered(i):
+        return jnp.concatenate([slabs[i, j] for j in range(owners)], axis=1)
+
+    def update(first):
         for b in range(blocks):
             work[:, block(b)] -= jnp.dot(first, sub_v[:, block(b)], preferred_element_type=jnp.float32)
 
-    coef[...] = reduce(1, total, update)
+    if not shared:
+        corr[...] = total
+    scatter(0, total)
+    if shared:
+        pl.when(jnp.logical_not(is_owner(me)))(functools.partial(arrive, 0))
+    else:
+        arrive(0)
+    first = gathered(0)
+    if not shared:
+        scatter(1, corr[...] - (
+            jnp.dot(first, gram_hi[...], preferred_element_type=jnp.float32)
+            + jnp.dot(first, gram_lo[...], preferred_element_type=jnp.float32)))
+    update(first)
+    arrive(1)
+    coef[...] = gathered(1)
 
     for s in range(2):
         pl.when(side == s)(functools.partial(close, s))
     for i in range(PASSES):
-        for_other_owners(lambda j: rs_copy(i, j).wait_send())
+        if not (shared and i):
+            for_other_owners(lambda j: rs_copy(i, j).wait_send())
 
         def sent():
             each(n - 1, lambda d: ag_copy(i, d).wait_send())
 
         pl.when(is_owner(me))(sent)
+    if shared:
+        for k in range(2):
+            tree_copy(k, twin).wait_send()
+        for_own_diag(lambda t: diag_copy(t).wait_send())
+
+        def inner_sent():
+            tree_copy(4, toward).wait_send()
+            pair_copy(strips.at[root], 0).wait_send()
+            pl.when((me - base) // 2 == root)(lambda: pair_copy(diag, 1).wait_send())
+
+        def outer_sent():
+            for k in range(2):
+                tree_copy(2 + k, toward).wait_send()
+
+        pl.when(is_owner(me))(inner_sent)
+        pl.when(jnp.logical_not(is_owner(me)))(outer_sent)
 
 
 def finish(blk, work, sub_v, coef, out, out_v, out_sem):
@@ -258,14 +398,53 @@
     spans = subspace.shape[0]
     blk = inverses.shape[1]
     blocks = cols // blk
-    owners = min(n // 2, rows // SUBLANES)
-    slab = rows // owners
+    owners = min(n // 2, spans // LANES)
+    width = spans // owners
     hbm = pl.BlockSpec(memory_space=pl.ANY)
     smem = pl.BlockSpec(memory_space=pltpu.SMEM)
     vmem = pl.BlockSpec(memory_space=pltpu.VMEM)
     dma = pltpu.SemaphoreType.DMA
+    shared = roots == 2 and owners == 4 and n == 2 * owners
+    f32, bf16 = jnp.float32, jnp.bfloat16
+    if shared:
+        gram = {
+            "gram_sum": pltpu.VMEM((spans, spans // roots), f32),
+            "strips": pltpu.VMEM((roots, width, spans // roots), LINK),
+            "diag_out": pltpu.VMEM((2, SUBLANES, width), f32), "diag_in": pltpu.VMEM((n, SUBLANES, width), f32),
+            "diag": pltpu.VMEM((SUBLANES, width), f32),
+            "tree_out": pltpu.VMEM((5, width, spans // roots), LINK),
+            "tree_in": pltpu.VMEM((5, width, spans // roots), LINK),
+            "tree_send": dma((5,)), "tree_recv": dma((5,)), "diag_send": dma((2,)), "diag_recv": dma((n,)),
+            "pair_send": dma((2,)), "pair_recv": dma((2,)),
+        }
+        rounds = 1
+    else:
+        gram = {
+            "gram_sum": pltpu.VMEM((spans, spans), f32), "corr": pltpu.VMEM((rows, spans), f32),
+            "gram_hi": pltpu.VMEM((spans, spans), bf16), "gram_lo": pltpu.VMEM((spans, spans), bf16),
+        }
+        rounds = PASSES
+    scratch = {
+        "table": pltpu.VMEM((OFFS, blk, blk), bf16), "res_v": pltpu.VMEM((rows, cols), bf16),
+        "partial": pltpu.VMEM((rounds, owners, rows, width), LINK),
+        "inbox": pltpu.VMEM((rounds, n, rows, width), LINK),
+        "slabs": pltpu.VMEM((PASSES, owners, rows, width), bf16),
+        "load_sem": dma((3,)),
+        "hop_send": dma((1 + OFFS, CHUNKS)), "hop_recv": dma((OFFS, CHUNKS)),
+        "swap_send": dma((OFFS, CHUNKS)), "swap_recv": dma((OFFS, CHUNKS)),
+        "rs_send": dma((rounds, owners)), "rs_recv": dma((rounds, n)),
+        "ag_send": dma((PASSES, n)), "ag_recv": dma((PASSES, owners)),
+        **gram,
+    }
+    absent = dict.fromkeys(
+        ("gram_hi", "gram_lo", "corr", "strips", "diag_out", "diag_in", "diag", "tree_out", "tree_in",
+         "tree_send", "tree_recv", "diag_send", "diag_recv", "pair_send", "pair_recv"))
+
+    def body(off, listed, res, sub, inv, work, sub_v, coef, *refs):
+        kernel(n, roots, off, listed, res, sub, inv, work, sub_v, coef, **{**absent, **dict(zip(scratch, refs))})
+
     held = pl.pallas_call(
-        functools.partial(kernel, n, roots),
+        body,
         out_shape=(
             pltpu.VMEM((rows, cols), jnp.float32),
             pltpu.VMEM((spans, cols), jnp.bfloat16),
@@ -273,22 +452,7 @@
         ),
         in_specs=[smem, smem, hbm, hbm, hbm],
         out_specs=(vmem, vmem, vmem),
-        scratch_shapes=[
-            pltpu.VMEM((OFFS, blk, blk), jnp.bfloat16),
-            pltpu.VMEM((rows, cols), jnp.bfloat16),
-            pltpu.VMEM((spans, spans), jnp.float32),
-            pltpu.VMEM((spans, spans), jnp.bfloat16),
-            pltpu.VMEM((spans, spans), jnp.bfloat16),
-            pltpu.VMEM((rows, spans), jnp.float32),
-            pltpu.VMEM((PASSES, owners, slab, spans), LINK),
-            pltpu.VMEM((PASSES, n, slab, spans), LINK),
-            pltpu.VMEM((PASSES, owners, slab, spans), jnp.bfloat16),
-            dma((3,)),
-            dma((1 + OFFS, CHUNKS)), dma((OFFS, CHUNKS)),
-            dma((OFFS, CHUNKS)), dma((OFFS, CHUNKS)),
-            dma((PASSES, owners)), dma((PASSES, n)),
-            dma((PASSES, n)), dma((PASSES, owners)),
-        ],
+        scratch_shapes=list(scratch.values()),
         compiler_params=pltpu.CompilerParams(
             collective_id=0, has_side_effects=True, vmem_limit_bytes=VMEM_GRANT),
     )(owner_offset, listed, residual, subspace, inverses)

time: 43.2 us -> 40.9 us (0.947)
  Pallas kernels: 43.1 us -> 40.7 us
    pallas_call x1, Pallas kernels: 41.5 us -> 39.1 us  [per_device(): pl.pallas_call(body, out_shape=(pltpu.VMEM((rows, cols), jnp.float32), pl...]
where the time goes in v2:
time: 40.9 us; the launch traced here: 40.7 us
  Pallas kernels  40.7 us (100%)
    pallas_call x1, Pallas kernels, per_device(): pl.pallas_call(body, out_shape=(pltpu.VMEM((rows, cols), jnp.float32), pl...  39.1 us
    pallas_call x1, Pallas kernels, per_device(): pl.pallas_call(functools.partial(finish, blk), out_shape=jax.ShapeDtypeSt...  1.57 us

profile of v2, /device:TPU:0, one launch (start us, length us, event | category | flops | bytes accessed | tf_op | source)
XLA Modules:
  0.0 40.7 jit_solution(6886454140286447476)
XLA Ops:
  0.0 39.1 %shard_map.55 = (f32[64,4096]{1,0:T(8,128)S(1)}, bf16[512,4096]{1,0:T(8,128)(2,1)S(1)}, bf16[64,512]{1,0:T(8,128)(2,1)S(1)}) custom-call(s32[8]{0:T(128)} %off.1, s32[8]{0:T(128)} %listed.1, bf16[64,4096]{1,0:T(8,128)(2,1)} %res.1, bf16[512,4096]{1,0:T(8,128)(2,1)} %sub.1, bf16[1,512,512]{2,1,0:T(8,128)(2,1)} %inv.1), custom_call_target="tpu_custom_call" | custom-call | tf_op jit(solution)/shard_map/pallas_call | solution.py:446
  39.1 1.6 %shard_map.56 = f32[64,4096]{1,0:T(8,128)} custom-call(f32[64,4096]{1,0:T(8,128)S(1)} %get-tuple-element.8.work, bf16[512,4096]{1,0:T(8,128)(2,1)S(1)} %get-tuple-element.9.sub_v, bf16[64,512]{1,0:T(8,128)(2,1)S(1)} %get-tuple-element.10.coef), custom_call_target="tpu_custom_call" | custom-call | tf_op jit(solution)/shard_map/pallas_call | solution.py:459

commit v3 on v2

--- a/solution.py
+++ b/solution.py
@@ -12,9 +12,12 @@
 SUBLANES = 8
 LANES = 128
 CHUNKS = 8
-EARLY = 3
-TREE_AT = 19
-TWINS_AT = 26
+LOW = 0
+BOTH = 4
+CROSS = 3
+LEAD = 3.5
+TREE_AT = 23
+TWINS_AT = 32
 MESH = pl.DeviceIdType.MESH
 VMEM_GRANT = 61_700_000
 
@@ -28,24 +31,31 @@
 
 
 def flows(side):
-    every, early, late = range(CHUNKS), range(EARLY), range(EARLY, CHUNKS)
+    every, low, both, high = range(CHUNKS), range(LOW), range(LOW, LOW + BOTH), range(LOW + BOTH, CHUNKS)
+    crossing = range(CHUNKS - CROSS, CHUNKS)
+    due = []
+
+    def arrive(start, chunks, slot, *targets):
+        for i, q in enumerate(chunks):
+            due.append((start + i, slot, q, [(there, peer) for there, peer, among in targets if q in among]))
+
     if side == 0:
-        own = [(every, 2, "near"), ]
-        order = []
-        for q in every:
-            order.append((2, q, [(1, "twin")]))
-            if q in early:
-                order.append((1, q, [(3, "near")]))
-        order += [(1, q, []) for q in late]
-        order += [(3, q, [(2, "twin")]) for q in early]
-        order += [(3, q, []) for q in late]
+        own = [(every, 2, "near")]
+        arrive(0, every, 2, (1, "twin", every), (3, "cross", crossing))
+        arrive(0.5, every, 1, (3, "near", range(LOW + BOTH)))
+        arrive(CHUNKS, low, 3, (2, "twin", every))
+        arrive(CHUNKS, both, 3)
+        arrive(CHUNKS, high, 3)
     else:
-        own = [(every, 1, "twin"), (late, 2, "near")]
-        order = [(2, q, [(3, "twin")]) for q in late]
-        order += [(1, q, [(3, "near")]) for q in every]
-        order += [(2, q, []) for q in early]
-        order += [(3, q, []) for q in every]
-    return own, order
+        own = [(every, 1, "twin"), (high, 2, "near"), (both, 2, "near")]
+        arrive(0, high, 2, (3, "twin", every))
+        arrive(len(high), both, 2)
+        arrive(LEAD, every, 1, (3, "near", range(CHUNKS - CROSS)))
+        arrive(CHUNKS + LEAD, low, 2)
+        arrive(CHUNKS, range(CHUNKS - CROSS), 3)
+        arrive(CHUNKS + 2, crossing, 3)
+    due.sort(key=lambda event: event[0])
+    return own, [event[1:] for event in due]
 
 
 def dot_t(a, b):
@@ -85,7 +95,7 @@
 
     side = lax.rem(me, 2)
     twin = me + 1 - 2 * side
-    peers = {"twin": twin, "near": lax.rem(me + n - 2, n)}
+    peers = {"twin": twin, "near": lax.rem(me + n - 2, n), "cross": lax.rem(me + n - 1, n)}
 
     barrier = pltpu.get_barrier_semaphore()
 
@@ -135,6 +145,7 @@
 
     lower = me < n // 2
     toward = jnp.where(lower, me + 2, me - 2)
+    beyond = jnp.where(lower, me + 4, me - 4)
 
     def strip(k, beside=False):
         owner = (1 - side if beside else side) + 2 * k
@@ -179,30 +190,34 @@
             tree_copy(k, twin).start()
         for_own_diag(lambda t: diag_copy(t).start())
 
+    def half_rows(far):
+        k = lower.astype(jnp.int32) if far else 1 - lower.astype(jnp.int32)
+        return pl.ds(pl.multiple_of((side + 2 * k) * width, width), width)
+
     def sum_twins():
         for k in range(2):
             tree_copy(k, twin).wait_recv()
             gram_sum[strip(k), :] += tree_in[k].astype(jnp.float32)
 
         def outer():
-            for k in range(2):
-                tree_out[2 + k] = gram_sum[strip(k), :].astype(LINK)
-                tree_copy(2 + k, toward).start()
+            tree_out[3] = gram_sum[half_rows(True), :].astype(LINK)
+            tree_copy(3, beyond).start()
+            tree_out[2] = gram_sum[half_rows(False), :].astype(LINK)
+            tree_copy(2, toward).start()
+
+        def inner():
+            tree_out[4] = gram_sum[half_rows(True), :].astype(LINK)
+            tree_copy(4, toward).start()
 
         pl.when(jnp.logical_not(is_owner(me)))(outer)
-
-    def sum_outer():
-        for k in range(2):
-            tree_copy(2 + k, toward).wait_recv()
-            gram_sum[strip(k), :] += tree_in[2 + k].astype(jnp.float32)
-        far = pl.ds(pl.multiple_of((side + 2 * lower.astype(jnp.int32)) * width, width), width)
-        tree_out[4] = gram_sum[far, :].astype(LINK)
-        tree_copy(4, toward).start()
+        pl.when(is_owner(me))(inner)
 
     def sum_inner():
-        tree_copy(4, toward).wait_recv()
-        near = pl.ds(pl.multiple_of((me - base) * width, width), width)
-        strips[root] = (gram_sum[near, :] + tree_in[4].astype(jnp.float32)).astype(LINK)
+        total = gram_sum[half_rows(False), :]
+        for k in (4, 2, 3):
+            tree_copy(k, toward).wait_recv()
+            total += tree_in[k].astype(jnp.float32)
+        strips[root] = total.astype(LINK)
         pair_copy(strips.at[root], 0).start()
 
         def sum_diag():
@@ -231,8 +246,8 @@
             if shared and i == TWINS_AT:
                 sum_twins()
             relay(e, q, e, "twin", 0).wait_recv()
-            for slot, peer in targets:
-                relay(e, q, slot, peer, 1 + e).start()
+            for j, (slot, peer) in enumerate(targets):
+                relay(e, q, slot, peer, 2 + e if j == 0 else 2 + OFFS).start()
             swap(e, q, root).start()
 
     def close(s):
@@ -241,8 +256,8 @@
             for q in chunks:
                 own_hop(q, slot, peer, j).wait_send()
         for e, q, targets in order:
-            for slot, peer in targets:
-                relay(e, q, slot, peer, 1 + e).wait_send()
+            for j, (slot, peer) in enumerate(targets):
+                relay(e, q, slot, peer, 2 + e if j == 0 else 2 + OFFS).wait_send()
             swap(e, q, root).wait_send()
 
     for s in range(2):
@@ -302,8 +317,6 @@
         each(n - 1, lambda d: ag_copy(i, d).start())
 
     def own_sum(i):
-        if shared:
-            sum_outer()
         inbox[i, me] = partial[i, me - base]
         each(n - 1, lambda d: rs_in(i, lax.rem(me + d + 1, n)).wait_recv())
         total = jnp.sum(inbox[i].astype(jnp.float32), axis=0)
@@ -322,6 +335,8 @@
         for j in range(owners):
             partial[i, j] = total[:, j * width:(j + 1) * width].astype(partial.dtype)
         for_other_owners(lambda j: rs_copy(i, j).start())
+        if shared and TWINS_AT >= 3 * CHUNKS + blocks:
+            sum_twins()
         pl.when(is_owner(me))(functools.partial(own_sum, i))
 
     def arrive(i):
@@ -371,8 +386,8 @@
             pl.when((me - base) // 2 == root)(lambda: pair_copy(diag, 1).wait_send())
 
         def outer_sent():
-            for k in range(2):
-                tree_copy(2 + k, toward).wait_send()
+            tree_copy(2, toward).wait_send()
+            tree_copy(3, beyond).wait_send()
 
         pl.when(is_owner(me))(inner_sent)
         pl.when(jnp.logical_not(is_owner(me)))(outer_sent)
@@ -430,7 +445,7 @@
         "inbox": pltpu.VMEM((rounds, n, rows, width), LINK),
         "slabs": pltpu.VMEM((PASSES, owners, rows, width), bf16),
         "load_sem": dma((3,)),
-        "hop_send": dma((1 + OFFS, CHUNKS)), "hop_recv": dma((OFFS, CHUNKS)),
+        "hop_send": dma((OFFS + 3, CHUNKS)), "hop_recv": dma((OFFS, CHUNKS)),
         "swap_send": dma((OFFS, CHUNKS)), "swap_recv": dma((OFFS, CHUNKS)),
         "rs_send": dma((rounds, owners)), "rs_recv": dma((rounds, n)),
         "ag_send": dma((PASSES, n)), "ag_recv": dma((PASSES, owners)),

time: 40.9 us -> 37.6 us (0.919)
  Pallas kernels: 40.7 us -> 37.5 us
    pallas_call x1, Pallas kernels: 39.1 us -> 35.9 us  [per_device(): pl.pallas_call(body, out_shape=(pltpu.VMEM((rows, cols), jnp.float32), pl...]
where the time goes in v3:
time: 37.6 us; the launch traced here: 37.5 us
  Pallas kernels  37.5 us (100%)
    pallas_call x1, Pallas kernels, per_device(): pl.pallas_call(body, out_shape=(pltpu.VMEM((rows, cols), jnp.float32), pl...  35.9 us
    pallas_call x1, Pallas kernels, per_device(): pl.pallas_call(functools.partial(finish, blk), out_shape=jax.ShapeDtypeSt...  1.57 us

profile of v3, /device:TPU:0, one launch (start us, length us, event | category | flops | bytes accessed | tf_op | source)
XLA Modules:
  0.0 37.5 jit_solution(13283025337893531494)
XLA Ops:
  0.0 35.9 %shard_map.55 = (f32[64,4096]{1,0:T(8,128)S(1)}, bf16[512,4096]{1,0:T(8,128)(2,1)S(1)}, bf16[64,512]{1,0:T(8,128)(2,1)S(1)}) custom-call(s32[8]{0:T(128)} %off.1, s32[8]{0:T(128)} %listed.1, bf16[64,4096]{1,0:T(8,128)(2,1)} %res.1, bf16[512,4096]{1,0:T(8,128)(2,1)} %sub.1, bf16[1,512,512]{2,1,0:T(8,128)(2,1)} %inv.1), custom_call_target="tpu_custom_call" | custom-call | tf_op jit(solution)/shard_map/pallas_call | solution.py:461
  35.9 1.6 %shard_map.56 = f32[64,4096]{1,0:T(8,128)} custom-call(f32[64,4096]{1,0:T(8,128)S(1)} %get-tuple-element.8.work, bf16[512,4096]{1,0:T(8,128)(2,1)S(1)} %get-tuple-element.9.sub_v, bf16[64,512]{1,0:T(8,128)(2,1)S(1)} %get-tuple-element.10.coef), custom_call_target="tpu_custom_call" | custom-call | tf_op jit(solution)/shard_map/pallas_call | solution.py:474

commit v4 on v3

--- a/solution.py
+++ b/solution.py
@@ -17,7 +17,6 @@
 CROSS = 3
 LEAD = 3.5
 TREE_AT = 23
-TWINS_AT = 32
 MESH = pl.DeviceIdType.MESH
 VMEM_GRANT = 61_700_000
 
@@ -243,8 +242,6 @@
                 gram_step(i)
             if shared and i == TREE_AT:
                 start_tree()
-            if shared and i == TWINS_AT:
-                sum_twins()
             relay(e, q, e, "twin", 0).wait_recv()
             for j, (slot, peer) in enumerate(targets):
                 relay(e, q, slot, peer, 2 + e if j == 0 else 2 + OFFS).start()
@@ -262,9 +259,7 @@
 
     for s in range(2):
         pl.when(side == s)(functools.partial(exchange, s))
-    if shared:
-        pass
-    else:
+    if not shared:
         high = gram_sum[...].astype(jnp.bfloat16)
         gram_hi[...] = high
         gram_lo[...] = (gram_sum[...] - high.astype(jnp.float32)).astype(jnp.bfloat16)
@@ -274,16 +269,6 @@
         for q in range(CHUNKS):
             swap(e, q, 1 - root).wait_recv()
 
-    total = jnp.zeros((rows, spans), jnp.float32)
-    for b in range(blocks):
-        x = res_v[:, block(b)]
-        solved = jnp.dot(x, table[off[b]], preferred_element_type=jnp.float32)
-        kept = jnp.where(listed[b] > 0, solved, x.astype(jnp.float32))
-        work[:, block(b)] = kept
-        total += dot_t(kept.astype(jnp.bfloat16), sub_v[:, block(b)])
-        if shared and b == TWINS_AT - 3 * CHUNKS:
-            sum_twins()
-
     def rs_copy(i, j):
         return pltpu.make_async_remote_copy(
             src_ref=partial.at[i, j], dst_ref=inbox.at[i, me],
@@ -296,11 +281,11 @@
             send_sem=rs_send.at[i, 0], recv_sem=rs_recv.at[i, peer],
             device_id={"tr": peer}, device_id_type=MESH)
 
-    def ag_copy(i, d):
+    def ag_copy(i, peer):
         return pltpu.make_async_remote_copy(
             src_ref=slabs.at[i, me - base], dst_ref=slabs.at[i, me - base],
-            send_sem=ag_send.at[i, d], recv_sem=ag_recv.at[i, me - base],
-            device_id={"tr": lax.rem(me + d + 1, n)}, device_id_type=MESH)
+            send_sem=ag_send.at[i, peer], recv_sem=ag_recv.at[i, me - base],
+            device_id={"tr": peer}, device_id_type=MESH)
 
     def ag_in(i, j):
         return pltpu.make_async_remote_copy(
@@ -308,13 +293,17 @@
             send_sem=ag_send.at[i, 0], recv_sem=ag_recv.at[i, j],
             device_id={"tr": base + j}, device_id_type=MESH)
 
+    def rest(d):
+        return lax.rem(base + owners + d, n)
+
     def for_other_owners(body):
         for j in range(owners):
             pl.when(me != base + j)(functools.partial(body, j))
 
     def send_slab(i, value):
         slabs[i, me - base] = value
-        each(n - 1, lambda d: ag_copy(i, d).start())
+        for_other_owners(lambda j: ag_copy(i, base + j).start())
+        each(n - owners, lambda d: ag_copy(i, rest(d)).start())
 
     def own_sum(i):
         inbox[i, me] = partial[i, me - base]
@@ -323,56 +312,97 @@
         send_slab(i, total.astype(jnp.bfloat16))
         if shared:
             sum_inner()
-            arrive(i)
-            first = gathered(i)
+            for k in range(2):
+                arrive(i, k)
+            first = all_gathered(i)
             paired()
             again = sum(
                 dot_t(first[:, h * half:(h + 1) * half], strips[h]) for h in range(roots))
             own = slabs[i, me - base].astype(jnp.float32)
             send_slab(i + 1, (total - (again + own * diag[pl.ds(0, 1), :])).astype(jnp.bfloat16))
 
-    def scatter(i, total):
-        for j in range(owners):
-            partial[i, j] = total[:, j * width:(j + 1) * width].astype(partial.dtype)
-        for_other_owners(lambda j: rs_copy(i, j).start())
-        if shared and TWINS_AT >= 3 * CHUNKS + blocks:
-            sum_twins()
-        pl.when(is_owner(me))(functools.partial(own_sum, i))
-
-    def arrive(i):
-        for_other_owners(lambda j: ag_in(i, j).wait_recv())
-
-    def gathered(i):
-        return jnp.concatenate([slabs[i, j] for j in range(owners)], axis=1)
+    group = owners // 2
+    reach = group * width
+    near_group = jnp.where(me < n // 2, 0, 1)
+    far_group = 1 - near_group
+
+    def reach_of(k):
+        return pl.ds(k * reach, reach) if isinstance(k, int) else pl.ds(pl.multiple_of(k * reach, reach), reach)
+
+    def scatter(i, k, total):
+        for t in range(group):
+            j = k * group + t
+            partial[i, j] = total[:, t * width:(t + 1) * width].astype(partial.dtype)
+            pl.when(me != base + j)(rs_copy(i, j).start)
+
+    def arrive(i, k):
+        for t in range(group):
+            j = k * group + t
+            pl.when(me != base + j)(ag_in(i, j).wait_recv)
+
+    def gathered(i, k):
+        return jnp.concatenate([slabs[i, k * group + t] for t in range(group)], axis=1)
+
+    def all_gathered(i):
+        return jnp.concatenate([gathered(i, k) for k in range(2)], axis=1)
 
     def update(first):
         for b in range(blocks):
             work[:, block(b)] -= jnp.dot(first, sub_v[:, block(b)], preferred_element_type=jnp.float32)
 
+    for stage, k in enumerate((far_group, near_group)):
+        total = jnp.zeros((rows, reach), jnp.float32)
+        for b in range(blocks):
+            if stage == 0:
+                x = res_v[:, block(b)]
+                solved = jnp.dot(x, table[off[b]], preferred_element_type=jnp.float32)
+                kept = jnp.where(listed[b] > 0, solved, x.astype(jnp.float32))
+                work[:, block(b)] = kept
+                rounded = kept.astype(jnp.bfloat16)
+                res_v[:, block(b)] = rounded
+            else:
+                rounded = res_v[:, block(b)]
+            total += dot_t(rounded, sub_v[reach_of(k), block(b)])
+        if not shared:
+            corr[:, reach_of(k)] = total
+        scatter(0, k, total)
+    if shared:
+        sum_twins()
+    pl.when(is_owner(me))(functools.partial(own_sum, 0))
+
+    def arrive_all(i):
+        for k in range(2):
+            arrive(i, k)
+
+    if shared:
+        pl.when(jnp.logical_not(is_owner(me)))(functools.partial(arrive_all, 0))
+    else:
+        arrive_all(0)
+    first = all_gathered(0)
     if not shared:
-        corr[...] = total
-    scatter(0, total)
-    if shared:
-        pl.when(jnp.logical_not(is_owner(me)))(functools.partial(arrive, 0))
-    else:
-        arrive(0)
-    first = gathered(0)
-    if not shared:
-        scatter(1, corr[...] - (
+        total = corr[...] - (
             jnp.dot(first, gram_hi[...], preferred_element_type=jnp.float32)
-            + jnp.dot(first, gram_lo[...], preferred_element_type=jnp.float32)))
+            + jnp.dot(first, gram_lo[...], preferred_element_type=jnp.float32))
+        for k in range(2):
+            scatter(1, k, total[:, k * reach:(k + 1) * reach])
+        pl.when(is_owner(me))(functools.partial(own_sum, 1))
     update(first)
-    arrive(1)
-    coef[...] = gathered(1)
-
     for s in range(2):
         pl.when(side == s)(functools.partial(close, s))
+    arrive(1, near_group)
+    near = gathered(1, near_group)
+    for b in range(blocks):
+        work[:, block(b)] -= jnp.dot(near, sub_v[reach_of(near_group), block(b)], preferred_element_type=jnp.float32)
+    arrive(1, far_group)
+    coef[...] = gathered(1, far_group)
+
     for i in range(PASSES):
         if not (shared and i):
             for_other_owners(lambda j: rs_copy(i, j).wait_send())
 
         def sent():
-            each(n - 1, lambda d: ag_copy(i, d).wait_send())
+            for_other_owners(lambda j: ag_copy(i, base + j).wait_send())
+            each(n - owners, lambda d: ag_copy(i, rest(d)).wait_send())
 
         pl.when(is_owner(me))(sent)
     if shared:
@@ -393,8 +423,10 @@
         pl.when(jnp.logical_not(is_owner(me)))(outer_sent)
 
 
-def finish(blk, work, sub_v, coef, out, out_v, out_sem):
+def finish(n, blk, work, sub_v, coef, out, out_v, out_sem):
     blocks = work.shape[1] // blk
+    reach = coef.shape[1]
+    far = pl.ds(pl.multiple_of(jnp.where(lax.axis_index("tr") < n // 2, 1, 0) * reach, reach), reach)
 
     def store(b):
         cols = pl.ds(b * blk, blk)
@@ -402,7 +434,7 @@
 
     for b in range(blocks):
         cols = pl.ds(b * blk, blk)
-        out_v[:, cols] = work[:, cols] - jnp.dot(coef[...], sub_v[:, cols], preferred_element_type=jnp.float32)
+        out_v[:, cols] = work[:, cols] - jnp.dot(coef[...], sub_v[far, cols], preferred_element_type=jnp.float32)
         store(b).start()
     for b in range(blocks):
         store(b).wait()
@@ -463,7 +495,7 @@
         out_shape=(
             pltpu.VMEM((rows, cols), jnp.float32),
             pltpu.VMEM((spans, cols), jnp.bfloat16),
-            pltpu.VMEM((rows, spans), jnp.bfloat16),
+            pltpu.VMEM((rows, spans // 2), jnp.bfloat16),
         ),
         in_specs=[smem, smem, hbm, hbm, hbm],
         out_specs=(vmem, vmem, vmem),
@@ -472,7 +504,7 @@
             collective_id=0, has_side_effects=True, vmem_limit_bytes=VMEM_GRANT),
     )(owner_offset, listed, residual, subspace, inverses)
     return pl.pallas_call(
-        functools.partial(finish, blk),
+        functools.partial(finish, n, blk),
         out_shape=jax.ShapeDtypeStruct((rows, cols), jnp.float32),
         in_specs=[vmem, vmem, vmem],
         out_specs=hbm,

time: 37.6 us -> 36.7 us (0.976)
  Pallas kernels: 37.5 us -> 36.5 us
    pallas_call x1, Pallas kernels: 35.9 us -> 35.3 us  [per_device(): pl.pallas_call(body, out_shape=(pltpu.VMEM((rows, cols), jnp.float32), pl...]
where the time goes in v4:
time: 36.7 us; the launch traced here: 36.6 us
  Pallas kernels  36.5 us (99%)
    pallas_call x1, Pallas kernels, per_device(): pl.pallas_call(body, out_shape=(pltpu.VMEM((rows, cols), jnp.float32), pl...  35.3 us
    pallas_call x1, Pallas kernels, per_device(): pl.pallas_call(functools.partial(finish, n, blk), out_shape=jax.ShapeDtyp...  1.26 us

profile of v4, /device:TPU:0, one launch (start us, length us, event | category | flops | bytes accessed | tf_op | source)
XLA Modules:
  0.0 36.6 jit_solution(18209659958616870937)
XLA Ops:
  0.0 35.3 %shard_map.55 = (f32[64,4096]{1,0:T(8,128)S(1)}, bf16[512,4096]{1,0:T(8,128)(2,1)S(1)}, bf16[64,256]{1,0:T(8,128)(2,1)S(1)}) custom-call(s32[8]{0:T(128)} %off.1, s32[8]{0:T(128)} %listed.1, bf16[64,4096]{1,0:T(8,128)(2,1)} %res.1, bf16[512,4096]{1,0:T(8,128)(2,1)} %sub.1, bf16[1,512,512]{2,1,0:T(8,128)(2,1)} %inv.1), custom_call_target="tpu_custom_call" | custom-call | tf_op jit(solution)/shard_map/pallas_call | solution.py:493
  35.3 1.3 %shard_map.56 = f32[64,4096]{1,0:T(8,128)} custom-call(f32[64,4096]{1,0:T(8,128)S(1)} %get-tuple-element.8.work, bf16[512,4096]{1,0:T(8,128)(2,1)S(1)} %get-tuple-element.9.sub_v, bf16[64,256]{1,0:T(8,128)(2,1)S(1)} %get-tuple-element.10.coef), custom_call_target="tpu_custom_call" | custom-call | tf_op jit(solution)/shard_map/pallas_call | solution.py:506

commit v5 on v4

--- a/solution.py
+++ b/solution.py
@@ -46,9 +46,9 @@
         arrive(CHUNKS, both, 3)
         arrive(CHUNKS, high, 3)
     else:
-        own = [(every, 1, "twin"), (high, 2, "near"), (both, 2, "near")]
-        arrive(0, high, 2, (3, "twin", every))
-        arrive(len(high), both, 2)
+        own = [(every, 1, "twin"), (both, 2, "near"), (high, 2, "near")]
+        arrive(len(both), high, 2, (3, "twin", every))
+        arrive(0, both, 2)
         arrive(LEAD, every, 1, (3, "near", range(CHUNKS - CROSS)))
         arrive(CHUNKS + LEAD, low, 2)
         arrive(CHUNKS, range(CHUNKS - CROSS), 3)
@@ -393,9 +393,6 @@
     near = gathered(1, near_group)
     for b in range(blocks):
         work[:, block(b)] -= jnp.dot(near, sub_v[reach_of(near_group), block(b)], preferred_element_type=jnp.float32)
-    arrive(1, far_group)
-    coef[...] = gathered(1, far_group)
-
     for i in range(PASSES):
         if not (shared and i):
             for_other_owners(lambda j: rs_copy(i, j).wait_send())
@@ -421,6 +418,9 @@
 
         pl.when(is_owner(me))(inner_sent)
         pl.when(jnp.logical_not(is_owner(me)))(outer_sent)
+
+    arrive(1, far_group)
+    coef[...] = gathered(1, far_group)
 
 
 def finish(n, blk, work, sub_v, coef, out, out_v, out_sem):

time: 36.7 us -> 36.7 us (level)
  no operation moved by 1% of the time
where the time goes in v5:
time: 36.7 us; the launch traced here: 36.6 us
  Pallas kernels  36.5 us (99%)
    pallas_call x1, Pallas kernels, per_device(): pl.pallas_call(body, out_shape=(pltpu.VMEM((rows, cols), jnp.float32), pl...  35.3 us
    pallas_call x1, Pallas kernels, per_device(): pl.pallas_call(functools.partial(finish, n, blk), out_shape=jax.ShapeDtyp...  1.26 us

profile of v5, /device:TPU:0, one launch (start us, length us, event | category | flops | bytes accessed | tf_op | source)
XLA Modules:
  0.0 36.6 jit_solution(2030671238830452349)
XLA Ops:
  0.0 35.3 %shard_map.55 = (f32[64,4096]{1,0:T(8,128)S(1)}, bf16[512,4096]{1,0:T(8,128)(2,1)S(1)}, bf16[64,256]{1,0:T(8,128)(2,1)S(1)}) custom-call(s32[8]{0:T(128)} %off.1, s32[8]{0:T(128)} %listed.1, bf16[64,4096]{1,0:T(8,128)(2,1)} %res.1, bf16[512,4096]{1,0:T(8,128)(2,1)} %sub.1, bf16[1,512,512]{2,1,0:T(8,128)(2,1)} %inv.1), custom_call_target="tpu_custom_call" | custom-call | tf_op jit(solution)/shard_map/pallas_call | solution.py:493
  35.3 1.3 %shard_map.56 = f32[64,4096]{1,0:T(8,128)} custom-call(f32[64,4096]{1,0:T(8,128)S(1)} %get-tuple-element.8.work, bf16[512,4096]{1,0:T(8,128)(2,1)S(1)} %get-tuple-element.9.sub_v, bf16[64,256]{1,0:T(8,128)(2,1)S(1)} %get-tuple-element.10.coef), custom_call_target="tpu_custom_call" | custom-call | tf_op jit(solution)/shard_map/pallas_call | solution.py:506
